TPU v7x, 256 devices: a whole 4x4x8 slice. The times are simulated.
256 devices in a mesh: dp: 16 (over z, core), expert: 16 (over y, x).
Axes of the slice: x: 4, y: 4, z: 8, core: 2. Of those that a mesh axis runs over, the one named last changes fastest.
Arguments:
- cotangent: bfloat16 [32768, 2048], P(('dp', 'expert')), may hold values from -6 to 6
- saved_gate_up: bfloat16 [32768, 8, 1536], P(('dp', 'expert')), may hold values from -6 to 6
- route_ids: int32 [32768, 8], P(('dp', 'expert')), may hold values from 0 to 31, all different within a row; in each aligned block of 128 rows (0 to 127, 128 to 255, ...) at most 64 rows name the same one
- route_weights: float32 [32768, 8], P(('dp', 'expert')), may hold values from 0.05 to 1
- w_down: bfloat16 [32, 768, 2048], P('expert', 'dp'), may hold values from -0.21875 to 0.21875
Outputs:
- grad_gate_up: bfloat16 [32768, 8, 1536], P(('dp', 'expert'))
- route_grad: float32 [32768, 8], P(('dp', 'expert'))
- grad_down: float32 [32, 768, 2048], P('expert', 'dp')
Inputs may be any that keep to these rules, and one draw needn't show every extreme that they name: `route_ids`: within the rows of one device (aligned blocks of 128 tokens), no expert is named by more than 64 routes, and in every draw some expert is named by exactly 64; the 8 experts of a token are distinct.
All inputs are finite; a program needn't handle non-finite values.
Results may differ from a plain program's by a relative error of at most 0.02.
Values may be sent and summed in bfloat16 or wider, within the bound.
A program may use at most 128 MiB of HBM per device.

v0:
```python
import jax
import jax.numpy as jnp
from jax import lax
from jax.sharding import PartitionSpec as P


def slot_counts(ids, experts):
    routes = ids.shape[-1]
    onehot = (ids[..., None] == jnp.arange(experts, dtype=jnp.int32)).astype(jnp.bfloat16)
    lower = (jnp.arange(routes)[:, None] > jnp.arange(routes)[None, :]).astype(jnp.bfloat16)
    before = jnp.einsum("rq,...qe->...re", lower, onehot, preferred_element_type=jnp.float32)
    return jnp.sum(before * onehot.astype(jnp.float32), axis=-1).astype(jnp.int32)


def local(cotangent, saved_gate_up, route_ids, route_weights, w_down):
    tokens, top = route_ids.shape
    width = cotangent.shape[1]
    hidden_units = saved_gate_up.shape[2] // 2
    owners = lax.axis_size("expert")
    replicas = lax.axis_size("dp")
    me = lax.axis_index("expert")
    local_experts = w_down.shape[0]
    experts = local_experts * owners
    capacity = min(tokens, 2 * tokens * top // experts)
    routes = tokens * top
    cot_group = lax.all_gather(cotangent, "expert", axis=0, tiled=True)
    ids_group = lax.all_gather(route_ids.reshape(1, routes), "expert", axis=0, tiled=True)
    full_down = lax.all_gather(w_down, "dp", axis=1, tiled=True)
    gate = saved_gate_up[:, :, :hidden_units].astype(jnp.float32)
    up = saved_gate_up[:, :, hidden_units:].astype(jnp.float32)
    sig = jax.nn.sigmoid(gate)
    act = gate * sig
    hidden = (act * up).astype(jnp.bfloat16)
    weights = route_weights[:, :, None]
    scaled = (weights * hidden.astype(jnp.float32)).astype(jnp.bfloat16)
    flat_ids = route_ids.reshape(routes)
    slot = slot_counts(flat_ids, experts)
    position = flat_ids * capacity + slot
    slot_ids = jnp.arange(experts * capacity, dtype=jnp.int32)
    match = position[None, :] == slot_ids[:, None]
    route_of_slot = jnp.sum(
        jnp.where(match, jnp.arange(routes, dtype=jnp.int32)[None, :], 0), axis=1
    )
    filled = jnp.any(match, axis=1)
    h_rows = jnp.where(
        filled[:, None],
        scaled.reshape(routes, hidden_units)[route_of_slot],
        jnp.zeros((), jnp.bfloat16),
    )
    h_send = h_rows.reshape(owners, local_experts, capacity, hidden_units)
    slot_all = slot_counts(ids_group, experts)
    mine = me * local_experts + jnp.arange(local_experts, dtype=jnp.int32)
    pos_all = ids_group * capacity + slot_all
    want = (mine[:, None] * capacity + jnp.arange(capacity, dtype=jnp.int32)[None, :]).reshape(-1)
    hit = pos_all[:, None, :] == want[None, :, None]
    token_of = jnp.sum(
        jnp.where(hit, (jnp.arange(routes, dtype=jnp.int32) // top)[None, None, :], 0), axis=2
    )
    rows = (jnp.arange(owners, dtype=jnp.int32)[:, None] * tokens + token_of).reshape(
        owners, local_experts, capacity
    )
    rows = jnp.transpose(rows, (1, 0, 2)).reshape(local_experts, owners * capacity)
    dy_recv = cot_group[rows]
    h_recv = lax.all_to_all(h_send, "expert", split_axis=0, concat_axis=2, tiled=True)[0]
    grads = jnp.einsum(
        "jsd,jfd->jsf", dy_recv, full_down, preferred_element_type=jnp.float32
    ).astype(jnp.bfloat16)
    back = lax.all_to_all(
        grads.reshape(1, local_experts, owners * capacity, hidden_units),
        "expert",
        split_axis=2,
        concat_axis=0,
        tiled=True,
    )
    parts = []
    for j in range(local_experts):
        part = jnp.einsum(
            "sf,sd->fd", h_recv[j], dy_recv[j], preferred_element_type=jnp.float32
        ).astype(jnp.bfloat16)
        parts.append(
            lax.psum_scatter(part, "dp", scatter_dimension=0, tiled=True).astype(jnp.float32)
        )
    grad_down = jnp.stack(parts)
    returned_rows = back.reshape(experts * capacity, hidden_units)[position]
    qf = returned_rows.reshape(tokens, top, hidden_units).astype(jnp.float32)
    route_grad = jnp.sum(qf * hidden.astype(jnp.float32), -1)
    d_hidden = weights * qf
    d_gate = d_hidden * up * sig * (1.0 + gate * (1.0 - sig))
    d_up = d_hidden * act
    grad_gate_up = jnp.concatenate([d_gate, d_up], -1).astype(jnp.bfloat16)
    return (grad_gate_up, route_grad, grad_down)


def solution(mesh):
    return jax.shard_map(
        local,
        mesh=mesh,
        in_specs=(
            P(("dp", "expert"), None),
            P(("dp", "expert"), None, None),
            P(("dp", "expert"), None),
            P(("dp", "expert"), None),
            P("expert", "dp", None),
        ),
        out_specs=(
            P(("dp", "expert"), None, None),
            P(("dp", "expert"), None),
            P("expert", "dp", None),
        ),
        check_vma=False,
    )
```

profile of v0, /device:TPU:2, one launch (start us, length us, event | category | flops | bytes accessed | tf_op | source)
XLA Modules:
  0.0 409.4 jit_solution(11496074652841021074)
XLA Ops:
  7.2 0.0 all-gather.4.cloned.1.call-start
  7.2 0.7 all-gather.4.cloned.1.call-update
  7.9 0.0 all-gather.6.cloned.1.call-start
  7.9 0.7 all-gather.6.cloned.1.call-update
  8.7 0.8 copy.30
  9.4 0.1 reshape.205
  9.5 23.6 %all-gather = s32[16,1,1024]{2,1,0:T(1,128)S(1)} all-gather(s32[1,1,1024]{2,1,0:T(1,128)S(1)} %reshape.205), channel_id=1, replica_groups=mesh['dp'=16,'expert'=16] {'expert'}, dimensions={0}, use_global_device_ids=true | all-gather | bytes 69632 | tf_op jit(solution)/shard_map/all_gather | solution.py:27
  33.2 0.1 iota_add_fusion
  33.3 0.1 add.119
  33.4 1.4 fusion.27
  34.8 1.0 select_reduce_fusion.1
  35.8 0.1 reduce_sum.51
  35.9 0.1 add_bitcast_fusion
  36.0 0.1 reshape.171
  36.1 53.2 %all-gather.4.cloned.1.call-done = bf16[2048,2048]{1,0:T(8,128)(2,1)} async-done(((bf16[128,2048]{1,0:T(8,128)(2,1)}), bf16[2048,2048]{1,0:T(8,128)(2,1)}) %all-gather.4.cloned.1.call-update) | async-done | bytes 8388624 | tf_op jit(solution)/shard_map/all_gather | solution.py:26
  89.3 20.8 %gather_fusion = bf16[2048,2048]{1,0:T(8,128)(2,1)} fusion(bf16[2048,2048]{1,0:T(8,128)(2,1)} %all-gather.4.cloned.1.call-done, s32[2048]{0:T(1024)S(1)} %bitcast_clamp_fusion), kind=kCustom, calls=%fused_computation | custom fusion | bytes 16785408 | tf_op jit(solution)/shard_map/gather | solution.py:63
  110.1 26.9 %all-gather.6.cloned.1.call-done = bf16[2,768,2048]{2,1,0:T(8,128)(2,1)} async-done(((bf16[2,48,2048]{2,1,0:T(8,128)(2,1)}), bf16[2,768,2048]{2,1,0:T(8,128)(2,1)}) %all-gather.6.cloned.1.call-update) | async-done | bytes 6291472 | tf_op jit(solution)/shard_map/all_gather | solution.py:28
  136.9 11.0 %convert_bitcast_fusion = bf16[1,2,1024,768]{3,2,1,0:T(8,128)(2,1)S(1)} fusion(bf16[2,1024,2048]{2,1,0:T(8,128)(2,1)} %bitcast.55, bf16[2,768,2048]{2,1,0:T(8,128)(2,1)} %all-gather.6.cloned.1.call-done), kind=kOutput, calls=%fused_computation.38 | convolution fusion | flops 6444023808 | bytes 17825792 | tf_op jit(solution)/shard_map/jsd,jfd->jsf/dot_general | solution.py:65
  147.9 4.9 %copy.32 = bf16[1,2,1024,768]{3,1,0,2:T(2,128)(2,1)} copy(bf16[1,2,1024,768]{3,2,1,0:T(8,128)(2,1)S(1)} %convert_bitcast_fusion) | data formatting | bytes 6291456 | tf_op jit(solution)/shard_map/reshape | solution.py:69
  152.8 7.4 %all-to-all-start = ((bf16[1,2,1024,768]{3,1,0,2:T(2,128)(2,1)}), bf16[1,2,1024,768]{3,1,0,2:T(2,128)(2,1)S(1)}, u32[]{:S(2)}, u32[]{:S(2)}) async-start(bf16[1,2,1024,768]{3,1,0,2:T(2,128)(2,1)} %copy.32), calls=%async_computation | async-start | bytes 6291456 | tf_op jit(solution)/shard_map/all_to_all | solution.py:68
  160.2 0.0 reduce-scatter.5.cloned.1.call-start
  160.3 0.1 eq.60
  160.4 0.1 copy.29
  160.5 0.1 copy.34
  160.6 0.1 mul.102
  160.7 0.5 fusion.31
  161.3 1.0 fusion
  162.3 0.1 broadcast_in_dim.36
  162.4 0.9 select_reduce_fusion
  163.4 41.3 %all-to-all-done = bf16[1,2,1024,768]{3,1,0,2:T(2,128)(2,1)S(1)} async-done(((bf16[1,2,1024,768]{3,1,0,2:T(2,128)(2,1)}), bf16[1,2,1024,768]{3,1,0,2:T(2,128)(2,1)S(1)}, u32[]{:S(2)}, u32[]{:S(2)}) %all-to-all-start) | async-done | bytes 3145760 | tf_op jit(solution)/shard_map/all_to_all | solution.py:68
  204.7 1.7 copy-done.1
  206.3 2.5 copy.33
  208.9 5.2 %gather_fusion.1 = bf16[1024,768]{1,0:T(8,128)(2,1)} fusion(bf16[2048,768]{1,0:T(8,128)(2,1)S(1)} %bitcast.51, s32[1024]{0:T(1024)S(1)} %broadcast_clamp_fusion.1), kind=kCustom, calls=%fused_computation.1 | custom fusion | bytes 3149824 | tf_op jit(solution)/shard_map/gather | solution.py:84
  214.1 5.0 %fusion.29 = (bf16[1024,768]{1,0:T(8,128)(2,1)S(1)}, bf16[128,8,768]{2,1,0:T(8,128)(2,1)S(1)}, bf16[128,8,768]{2,1,0:T(8,128)(2,1)}, bf16[128,8,768]{2,1,0:T(8,128)(2,1)}) fusion(f32[128,8]{1,0:T(8,128)S(1)} %copy.29, bf16[128,8,1536]{2,1,0:T(8,128)(2,1)} %param.6, bf16[1024,768]{1,0:T(8,128)(2,1)} %gather_fusion.1), kind=kLoop, calls=%fused_computation.44 | loop fusion | flops 17301504 | bytes 11014144 | tf_op jit(solution)/shard_map/reshape | solution.py:47
  219.0 9.4 %gather_fusion.2 = bf16[2048,768]{1,0:T(8,128)(2,1)} fusion(bf16[1024,768]{1,0:T(8,128)(2,1)S(1)} %get-tuple-element.9, s32[2048]{0:T(1024)S(1)} %broadcast_clamp_fusion), kind=kCustom, calls=%fused_computation.2 | custom fusion | bytes 6299648 | tf_op jit(solution)/shard_map/gather | solution.py:47
  228.4 2.3 broadcast_select_fusion
  230.7 46.5 %all_to_all.30 = bf16[16,2,64,768]{3,2,1,0:T(8,128)(2,1)S(1)} all-to-all(bf16[16,2,64,768]{3,2,1,0:T(8,128)(2,1)S(1)} %broadcast_select_fusion), channel_id=1, replica_groups=mesh['dp'=16,'expert'=16] {'expert'}, dimensions={0} | all-to-all | bytes 6291456 | tf_op jit(solution)/shard_map/all_to_all | solution.py:64
  277.2 0.2 fusion.42
  277.5 4.9 %fusion.13 = bf16[768,2048]{1,0:T(8,128)(2,1)} fusion(bf16[1024,768]{1,0:T(8,128)(2,1)S(1)} %bitcast.59, bf16[2048,2048]{1,0:T(8,128)(2,1)S(1)} %bitcast.57), kind=kOutput, calls=%fused_computation.25 | convolution fusion | flops 3222798336 | bytes 8912896 | tf_op jit(solution)/shard_map/sf,sd->fd/dot_general | solution.py:77
  282.4 0.0 reduce-scatter.3.cloned.1.call-start
  282.5 7.0 %fusion.10 = bf16[768,2048]{1,0:T(8,128)(2,1)} fusion(bf16[1024,768]{1,0:T(8,128)(2,1)S(1)} %bitcast.58, bf16[2048,2048]{1,0:T(8,128)(2,1)} %gather_fusion), kind=kOutput, calls=%fused_computation.24 | convolution fusion | flops 3222798336 | bytes 8912896 | tf_op jit(solution)/shard_map/sf,sd->fd/dot_general | solution.py:77
  289.6 1.4 copy-done
  290.9 0.5 fusion.22
  291.4 0.7 copy.36
  292.1 3.8 pad_maximum_fusion
  295.9 43.3 %reduce-scatter.5.cloned.1.call-done = bf16[48,2048]{1,0:T(8,128)(2,1)} async-done(((bf16[768,2048]{1,0:T(8,128)(2,1)}), bf16[48,2048]{1,0:T(8,128)(2,1)}) %reduce-scatter.5.cloned.1.call-update) | async-done | bytes 196624 | tf_op jit(solution)/shard_map/reduce_scatter | solution.py:81
  339.2 61.7 %reduce-scatter.3.cloned.1.call-done = bf16[48,2048]{1,0:T(8,128)(2,1)} async-done(((bf16[768,2048]{1,0:T(8,128)(2,1)}), bf16[48,2048]{1,0:T(8,128)(2,1)}) %reduce-scatter.3.cloned.1.call-update) | async-done | bytes 196624 | tf_op jit(solution)/shard_map/reduce_scatter | solution.py:81
  400.9 2.0 maximum_convert_fusion
  (28 shorter events, 0.2 us)
Async XLA Ops:
  7.2 82.1 %all-gather.4.cloned.1.call-start = ((), (), s32[]{:S(2)}) async-start(), calls=%async_computation.4 | async-start | bytes 8912896 | tf_op jit(solution)/shard_map/all_gather | solution.py:26
  7.9 129.0 %all-gather.6.cloned.1.call-start = ((), (), s32[]{:S(2)}) async-start(), calls=%async_computation.5 | async-start | bytes 6684672 | tf_op jit(solution)/shard_map/all_gather | solution.py:28
  152.8 7.5 %copy-start.3 = (f32[128,8]{0,1:T(8,128)S(1)}, f32[128,8]{0,1:T(8,128)}, u32[]{:S(2)}) copy-start(f32[128,8]{0,1:T(8,128)} %param.8) | copy-start | bytes 12292
  152.8 7.7 %copy-start.2 = (s32[128,8]{0,1:T(8,128)S(1)}, s32[128,8]{0,1:T(8,128)}, u32[]{:S(2)}) copy-start(s32[128,8]{0,1:T(8,128)} %param.7) | copy-start | bytes 12292
  152.8 51.8 %all-to-all-start = ((bf16[1,2,1024,768]{3,1,0,2:T(2,128)(2,1)}), bf16[1,2,1024,768]{3,1,0,2:T(2,128)(2,1)S(1)}, u32[]{:S(2)}, u32[]{:S(2)}) async-start(bf16[1,2,1024,768]{3,1,0,2:T(2,128)(2,1)} %copy.32), calls=%async_computation | async-start | bytes 6291456 | tf_op jit(solution)/shard_map/all_to_all | solution.py:68
  160.2 179.0 %reduce-scatter.5.cloned.1.call-start = ((), (), s32[]{:S(2)}) async-start(), calls=%async_computation.7 | async-start | bytes 3342336 | tf_op jit(solution)/shard_map/reduce_scatter | solution.py:81
  204.7 1.7 copy-start.1
  228.4 49.1 %slice-start = ((s8[8388608]{0:T(1024)(128)(4,1)}), s8[4194304]{0:T(1024)(128)(4,1)S(1)}, s32[]{:S(2)}) async-start(s8[8388608]{0:T(1024)(128)(4,1)} %bitcast.56), calls=%async_computation.8 | async-start | bytes 8388608
  230.7 46.8 %slice-start.1 = ((s8[8388608]{0:T(1024)(128)(4,1)}), s8[4194304]{0:T(1024)(128)(4,1)S(1)}, s32[]{:S(2)}) async-start(s8[8388608]{0:T(1024)(128)(4,1)} %bitcast.56), calls=%async_computation.9 | async-start | bytes 8388608
  282.4 118.5 %reduce-scatter.3.cloned.1.call-start = ((), (), s32[]{:S(2)}) async-start(), calls=%async_computation.6 | async-start | bytes 3342336 | tf_op jit(solution)/shard_map/reduce_scatter | solution.py:81
  289.5 1.4 copy-start
Sparse Core Ops, SparseCore 0:
  10.4 78.7 all-gather.3
  91.1 45.7 all-gather.5
  282.6 56.6 reduce-scatter.4
  341.6 59.2 reduce-scatter.2
where the time goes:
time: 410 us; the launch traced here: 409 us
  waiting for transfers between devices  228 us (56%)
  blocking collectives  70.2 us (17%)
  local copies, waits for them, and re-layouts  48.4 us (12%)
  matrix products  24.9 us (6%)
  other arithmetic  16.6 us (4%)
  between operations  14 us (3%)
  starting transfers between devices  7.56 us (2%)
    reduce_scatter x2, waiting for transfers between devices, local(): lax.psum_scatter(part, 'dp', scatter_dimension=0, tiled=True)  105 us
    all_gather x1, waiting for transfers between devices, local(): cot_group = lax.all_gather(cotangent, 'expert', axis=0, tiled=True)  53.2 us
    all_to_all x1, blocking collectives, local(): lax.all_to_all(h_send, 'expert', split_axis=0, concat_axis=2, tiled=True)[0]  46.5 us
    all_to_all x1, waiting for transfers between devices, local(): lax.all_to_all(grads.reshape(1, local_experts, owners * capacity, hidden_...  41.3 us
    all_gather x1, waiting for transfers between devices, local(): full_down = lax.all_gather(w_down, 'dp', axis=1, tiled=True)  26.9 us
    all_gather x1, blocking collectives, local(): lax.all_gather(route_ids.reshape(1, routes), 'expert', axis=0, tiled=True)  23.6 us
    gather x1, local copies, waits for them, and re-layouts, local(): dy_recv = cot_group[rows]  20.8 us
    dot_general x2, matrix products, local(): jnp.einsum('sf,sd->fd', h_recv[j], dy_recv[j], preferred_element_type=jnp...  11.9 us
  transfers between devices with their start and end apart: 5, of which 5 were waited for; matrix products, arithmetic and copies ran while one was open for 10% of the time, Pallas kernels for 0%

commit v1 on v0

--- a/solution.py
+++ b/solution.py
@@ -25,7 +25,21 @@
     routes = tokens * top
     cot_group = lax.all_gather(cotangent, "expert", axis=0, tiled=True)
     ids_group = lax.all_gather(route_ids.reshape(1, routes), "expert", axis=0, tiled=True)
-    full_down = lax.all_gather(w_down, "dp", axis=1, tiled=True)
+    ways, here, step = (lax.axis_size("dp"), lax.axis_index("dp"), w_down.shape[1])
+    dims = [n * ways if d == 1 else n for d, n in enumerate(w_down.shape)]
+    full = lax.dynamic_update_slice_in_dim(
+        jnp.zeros(dims, w_down.dtype), w_down, here * step, axis=1
+    )
+    going_up = going_down = w_down
+    for far in range(1, ways // 2 + 1):
+        going_up = lax.ppermute(going_up, "dp", [(d, (d + 1) % ways) for d in range(ways)])
+        full = lax.dynamic_update_slice_in_dim(full, going_up, (here - far) % ways * step, axis=1)
+        if 2 * far < ways:
+            going_down = lax.ppermute(going_down, "dp", [(d, (d - 1) % ways) for d in range(ways)])
+            full = lax.dynamic_update_slice_in_dim(
+                full, going_down, (here + far) % ways * step, axis=1
+            )
+    full_down = full
     gate = saved_gate_up[:, :, :hidden_units].astype(jnp.float32)
     up = saved_gate_up[:, :, hidden_units:].astype(jnp.float32)
     sig = jax.nn.sigmoid(gate)

time: 410 us -> 388 us (0.946)
  waiting for transfers between devices: 228 us -> 173 us
  starting transfers between devices: 7.56 us -> 30.9 us
  local copies, waits for them, and re-layouts: 48.4 us -> 64.8 us
  blocking collectives: 70.2 us -> 62.6 us
    all_gather x1, waiting for transfers between devices: 53.2 us -> 0.01 us  [local(): cot_group = lax.all_gather(cotangent, 'expert', axis=0, tiled=True)]
    ppermute x0 -> x15, waiting for transfers between devices: none -> 28.1 us  [the longest x8 25.5 us: local(): lax.ppermute(going_up, 'dp', [(d, (d + 1) % ways) for d in range(ways)])]
    all_gather x1 -> x0, waiting for transfers between devices: 26.9 us -> none  [local(): full_down = lax.all_gather(w_down, 'dp', axis=1, tiled=True)]
    ppermute x0 -> x15, starting transfers between devices: none -> 25.2 us  [the longest x7 25.1 us: local(): lax.ppermute(going_down, 'dp', [(d, (d - 1) % ways) for d in range(ways)])]
    dynamic_update_slice x0 -> x16, local copies, waits for them, and re-layouts: none -> 12.5 us  [the longest x8 6.27 us: local(): lax.dynamic_update_slice_in_dim(full, going_up, (here - far) % ways * ste...]
    all_to_all x1, waiting for transfers between devices: 41.3 us -> 31.8 us  [local(): lax.all_to_all(grads.reshape(1, local_experts, owners * capacity, hidden_...]
    reduce_scatter x2, waiting for transfers between devices: 105 us -> 113 us  [local(): lax.psum_scatter(part, 'dp', scatter_dimension=0, tiled=True)]
    all_to_all x1, blocking collectives: 46.5 us -> 39 us  [local(): lax.all_to_all(h_send, 'expert', split_axis=0, concat_axis=2, tiled=True)[0]]
  transfers between devices with their start and end apart: 5 -> 19, of which waited for: 5 -> 14; matrix products, arithmetic and copies ran while one was open for 10% -> 9% of each run, Pallas kernels for 0% -> 0%
where the time goes in v1:
time: 388 us; the launch traced here: 387 us
  waiting for transfers between devices  173 us (45%)
  local copies, waits for them, and re-layouts  64.8 us (17%)
  blocking collectives  62.6 us (16%)
  starting transfers between devices  30.9 us (8%)
  matrix products  24.9 us (6%)
  other arithmetic  16.6 us (4%)
  between operations  14 us (4%)
    reduce_scatter x2, waiting for transfers between devices, local(): lax.psum_scatter(part, 'dp', scatter_dimension=0, tiled=True)  113 us
    all_to_all x1, blocking collectives, local(): lax.all_to_all(h_send, 'expert', split_axis=0, concat_axis=2, tiled=True)[0]  39 us
    all_to_all x1, waiting for transfers between devices, local(): lax.all_to_all(grads.reshape(1, local_experts, owners * capacity, hidden_...  31.8 us
    ppermute x8, waiting for transfers between devices, local(): lax.ppermute(going_up, 'dp', [(d, (d + 1) % ways) for d in range(ways)])  25.5 us
    ppermute x7, starting transfers between devices, local(): lax.ppermute(going_down, 'dp', [(d, (d - 1) % ways) for d in range(ways)])  25.1 us
    all_gather x1, blocking collectives, local(): lax.all_gather(route_ids.reshape(1, routes), 'expert', axis=0, tiled=True)  23.7 us
    gather x1, local copies, waits for them, and re-layouts, local(): dy_recv = cot_group[rows]  21 us
    dot_general x2, matrix products, local(): jnp.einsum('sf,sd->fd', h_recv[j], dy_recv[j], preferred_element_type=jnp...  12 us
  transfers between devices with their start and end apart: 19, of which 14 were waited for; matrix products, arithmetic and copies ran while one was open for 9% of the time, Pallas kernels for 0%

profile of v1, /device:TPU:2, one launch (start us, length us, event | category | flops | bytes accessed | tf_op | source)
XLA Modules:
  0.0 387.2 jit_solution(13568853376171817681)
XLA Ops:
  7.9 5.3 %collective-permute-start.1 = (bf16[2,48,2048]{2,1,0:T(8,128)(2,1)}, bf16[2,48,2048]{2,1,0:T(8,128)(2,1)S(1)}, u32[]{:S(2)}, u32[]{:S(2)}) collective-permute-start(bf16[2,48,2048]{2,1,0:T(8,128)(2,1)} %param.9), channel_id=1, source_target_pairs={{0,240},{16,0},{32,16},{48,32},{64,48},{80,64},{96,80},{112,96},{1... | collective-permute-start | bytes 1179656 | tf_op jit(solution)/shard_map/ppermute | solution.py:38
  13.2 0.8 copy.30
  14.1 23.7 %all-gather = s32[16,1,1024]{2,1,0:T(1,128)S(1)} all-gather(s32[1,1,1024]{2,1,0:T(1,128)S(1)} %reshape.205), channel_id=1, replica_groups=mesh['dp'=16,'expert'=16] {'expert'}, dimensions={0}, use_global_device_ids=true | all-gather | bytes 69632 | tf_op jit(solution)/shard_map/all_gather | solution.py:27
  38.0 1.4 fusion.27
  39.4 1.0 select_reduce_fusion.1
  40.7 3.4 broadcast_in_dim.42
  44.2 0.8 constant_dynamic-update-slice_fusion.15
  45.0 3.0 collective-permute-start.3
  48.7 0.8 constant_dynamic-update-slice_fusion.13
  49.5 3.9 %collective-permute-done.2 = bf16[2,48,2048]{2,1,0:T(8,128)(2,1)S(1)} collective-permute-done((bf16[2,48,2048]{2,1,0:T(8,128)(2,1)S(1)}, bf16[2,48,2048]{2,1,0:T(8,128)(2,1)S(1)}, u32[]{:S(2)}, u32[]{:S(2)}) %collective-permute-start.2) | collective-permute-done | bytes 393248 | tf_op jit(solution)/shard_map/ppermute | solution.py:35
  53.4 3.0 collective-permute-start.5
  56.3 0.8 constant_dynamic-update-slice_fusion.12
  57.1 0.8 constant_dynamic-update-slice_fusion.11
  57.9 3.9 %collective-permute-done.4 = bf16[2,48,2048]{2,1,0:T(8,128)(2,1)S(1)} collective-permute-done((bf16[2,48,2048]{2,1,0:T(8,128)(2,1)S(1)}, bf16[2,48,2048]{2,1,0:T(8,128)(2,1)S(1)}, u32[]{:S(2)}, u32[]{:S(2)}) %collective-permute-start.4) | collective-permute-done | bytes 393248 | tf_op jit(solution)/shard_map/ppermute | solution.py:35
  61.8 3.4 collective-permute-start.7
  66.7 3.5 collective-permute-done.6
  70.4 3.5 collective-permute-start.9
  75.5 3.1 collective-permute-done.8
  79.2 3.5 collective-permute-start.11
  82.8 0.8 constant_dynamic-update-slice_fusion.6
  84.3 2.7 collective-permute-done.10
  87.0 1.0 collective-permute-done.11
  88.1 3.5 collective-permute-start.13
  92.4 0.8 constant_dynamic-update-slice_fusion.3
  93.2 2.3 collective-permute-done.12
  96.9 0.8 constant_dynamic-update-slice_fusion.1
  97.7 6.2 %collective-permute-done.14 = bf16[2,48,2048]{2,1,0:T(8,128)(2,1)S(1)} collective-permute-done((bf16[2,48,2048]{2,1,0:T(8,128)(2,1)S(1)}, bf16[2,48,2048]{2,1,0:T(8,128)(2,1)S(1)}, u32[]{:S(2)}, u32[]{:S(2)}) %collective-permute-start.14) | collective-permute-done | bytes 393248 | tf_op jit(solution)/shard_map/ppermute | solution.py:35
  104.6 21.0 %gather_fusion = bf16[2048,2048]{1,0:T(8,128)(2,1)} fusion(bf16[2048,2048]{1,0:T(8,128)(2,1)} %all-gather.3.cloned.1.call-done, s32[2048]{0:T(1024)S(1)} %bitcast_clamp_fusion), kind=kCustom, calls=%fused_computation | custom fusion | bytes 16785408 | tf_op jit(solution)/shard_map/gather | solution.py:77
  125.6 11.0 %convert_bitcast_fusion = bf16[1,2,1024,768]{3,2,1,0:T(8,128)(2,1)S(1)} fusion(bf16[2,1024,2048]{2,1,0:T(8,128)(2,1)} %bitcast.55, bf16[2,768,2048]{2,1,0:T(8,128)(2,1)} %constant_dynamic-update-slice_fusion), kind=kOutput, calls=%fused_computation.38 | convolution fusion | flops 6444023808 | bytes 17825792 | tf_op jit(solution)/shard_map/jsd,jfd->jsf/dot_general | solution.py:79
  136.6 4.9 %copy.32 = bf16[1,2,1024,768]{3,1,0,2:T(2,128)(2,1)} copy(bf16[1,2,1024,768]{3,2,1,0:T(8,128)(2,1)S(1)} %convert_bitcast_fusion) | data formatting | bytes 6291456 | tf_op jit(solution)/shard_map/reshape | solution.py:83
  141.5 5.6 %all-to-all-start = ((bf16[1,2,1024,768]{3,1,0,2:T(2,128)(2,1)}), bf16[1,2,1024,768]{3,1,0,2:T(2,128)(2,1)S(1)}, u32[]{:S(2)}, u32[]{:S(2)}) async-start(bf16[1,2,1024,768]{3,1,0,2:T(2,128)(2,1)} %copy.32), calls=%async_computation | async-start | bytes 6291456 | tf_op jit(solution)/shard_map/all_to_all | solution.py:82
  148.2 1.0 fusion
  149.3 0.9 select_reduce_fusion
  150.3 31.8 %all-to-all-done = bf16[1,2,1024,768]{3,1,0,2:T(2,128)(2,1)S(1)} async-done(((bf16[1,2,1024,768]{3,1,0,2:T(2,128)(2,1)}), bf16[1,2,1024,768]{3,1,0,2:T(2,128)(2,1)S(1)}, u32[]{:S(2)}, u32[]{:S(2)}) %all-to-all-start) | async-done | bytes 3145760 | tf_op jit(solution)/shard_map/all_to_all | solution.py:82
  182.0 1.7 copy-done.1
  183.7 2.5 copy.33
  186.2 5.5 %gather_fusion.1 = bf16[1024,768]{1,0:T(8,128)(2,1)} fusion(bf16[2048,768]{1,0:T(8,128)(2,1)S(1)} %bitcast.51, s32[1024]{0:T(1024)S(1)} %broadcast_clamp_fusion.1), kind=kCustom, calls=%fused_computation.1 | custom fusion | bytes 3149824 | tf_op jit(solution)/shard_map/gather | solution.py:98
  191.7 5.0 %fusion.29 = (bf16[1024,768]{1,0:T(8,128)(2,1)S(1)}, bf16[128,8,768]{2,1,0:T(8,128)(2,1)S(1)}, bf16[128,8,768]{2,1,0:T(8,128)(2,1)}, bf16[128,8,768]{2,1,0:T(8,128)(2,1)}) fusion(f32[128,8]{1,0:T(8,128)S(1)} %copy.29, bf16[128,8,1536]{2,1,0:T(8,128)(2,1)} %param.6, bf16[1024,768]{1,0:T(8,128)(2,1)} %gather_fusion.1), kind=kLoop, calls=%fused_computation.44 | loop fusion | flops 17301504 | bytes 11014144 | tf_op jit(solution)/shard_map/reshape | solution.py:61
  196.7 9.4 %gather_fusion.2 = bf16[2048,768]{1,0:T(8,128)(2,1)} fusion(bf16[1024,768]{1,0:T(8,128)(2,1)S(1)} %get-tuple-element.9, s32[2048]{0:T(1024)S(1)} %broadcast_clamp_fusion), kind=kCustom, calls=%fused_computation.2 | custom fusion | bytes 6299648 | tf_op jit(solution)/shard_map/gather | solution.py:61
  206.1 2.3 broadcast_select_fusion
  208.3 39.0 %all_to_all.30 = bf16[16,2,64,768]{3,2,1,0:T(8,128)(2,1)S(1)} all-to-all(bf16[16,2,64,768]{3,2,1,0:T(8,128)(2,1)S(1)} %broadcast_select_fusion), channel_id=1, replica_groups=mesh['dp'=16,'expert'=16] {'expert'}, dimensions={0} | all-to-all | bytes 6291456 | tf_op jit(solution)/shard_map/all_to_all | solution.py:78
  247.6 4.9 %fusion.13 = bf16[768,2048]{1,0:T(8,128)(2,1)} fusion(bf16[1024,768]{1,0:T(8,128)(2,1)S(1)} %bitcast.59, bf16[2048,2048]{1,0:T(8,128)(2,1)S(1)} %bitcast.57), kind=kOutput, calls=%fused_computation.25 | convolution fusion | flops 3222798336 | bytes 8912896 | tf_op jit(solution)/shard_map/sf,sd->fd/dot_general | solution.py:91
  252.6 7.1 %fusion.10 = bf16[768,2048]{1,0:T(8,128)(2,1)} fusion(bf16[1024,768]{1,0:T(8,128)(2,1)S(1)} %bitcast.58, bf16[2048,2048]{1,0:T(8,128)(2,1)} %gather_fusion), kind=kOutput, calls=%fused_computation.24 | convolution fusion | flops 3222798336 | bytes 8912896 | tf_op jit(solution)/shard_map/sf,sd->fd/dot_general | solution.py:91
  259.7 1.4 copy-done
  262.2 3.8 pad_maximum_fusion
  266.0 50.7 %reduce-scatter.5.cloned.1.call-done = bf16[48,2048]{1,0:T(8,128)(2,1)} async-done(((bf16[768,2048]{1,0:T(8,128)(2,1)}), bf16[48,2048]{1,0:T(8,128)(2,1)}) %reduce-scatter.5.cloned.1.call-update) | async-done | bytes 196624 | tf_op jit(solution)/shard_map/reduce_scatter | solution.py:95
  316.7 62.1 %reduce-scatter.3.cloned.1.call-done = bf16[48,2048]{1,0:T(8,128)(2,1)} async-done(((bf16[768,2048]{1,0:T(8,128)(2,1)}), bf16[48,2048]{1,0:T(8,128)(2,1)}) %reduce-scatter.3.cloned.1.call-update) | async-done | bytes 196624 | tf_op jit(solution)/shard_map/reduce_scatter | solution.py:95
  378.8 2.0 maximum_convert_fusion
  (74 shorter events, 12.4 us)
Async XLA Ops:
  7.2 97.5 %all-gather.3.cloned.1.call-start = ((), (), s32[]{:S(2)}) async-start(), calls=%async_computation.4 | async-start | bytes 8912896 | tf_op jit(solution)/shard_map/all_gather | solution.py:26
  7.9 37.1 %collective-permute-start = (bf16[2,48,2048]{2,1,0:T(8,128)(2,1)}, bf16[2,48,2048]{2,1,0:T(8,128)(2,1)S(1)}, u32[]{:S(2)}, u32[]{:S(2)}) collective-permute-start(bf16[2,48,2048]{2,1,0:T(8,128)(2,1)} %param.9), channel_id=1, source_target_pairs={{0,16},{16,32},{32,48},{48,64},{64,80},{80,96},{96,112},{112,128},... | collective-permute-start | bytes 1179656 | tf_op jit(solution)/shard_map/ppermute | solution.py:35
  7.9 37.0 %collective-permute-start.1 = (bf16[2,48,2048]{2,1,0:T(8,128)(2,1)}, bf16[2,48,2048]{2,1,0:T(8,128)(2,1)S(1)}, u32[]{:S(2)}, u32[]{:S(2)}) collective-permute-start(bf16[2,48,2048]{2,1,0:T(8,128)(2,1)} %param.9), channel_id=1, source_target_pairs={{0,240},{16,0},{32,16},{48,32},{64,48},{80,64},{96,80},{112,96},{1... | collective-permute-start | bytes 1179656 | tf_op jit(solution)/shard_map/ppermute | solution.py:38
  39.4 4.8 %copy-start.2 = (bf16[2,48,2048]{2,1,0:T(8,128)(2,1)S(1)}, bf16[2,48,2048]{2,1,0:T(8,128)(2,1)}, u32[]{:S(2)}) copy-start(bf16[2,48,2048]{2,1,0:T(8,128)(2,1)} %param.9) | copy-start | bytes 1179652
  45.0 8.4 %collective-permute-start.2 = (bf16[2,48,2048]{2,1,0:T(8,128)(2,1)S(1)}, bf16[2,48,2048]{2,1,0:T(8,128)(2,1)S(1)}, u32[]{:S(2)}, u32[]{:S(2)}) collective-permute-start(bf16[2,48,2048]{2,1,0:T(8,128)(2,1)S(1)} %collective-permute-done), channel_id=1, source_target_pairs={{0,16},{16,32},{32,48},{48,64},{64,80},{80,96},{96,112},{112,128},... | collective-permute-start | bytes 1179656 | tf_op jit(solution)/shard_map/ppermute | solution.py:35
  45.0 8.4 %collective-permute-start.3 = (bf16[2,48,2048]{2,1,0:T(8,128)(2,1)S(1)}, bf16[2,48,2048]{2,1,0:T(8,128)(2,1)S(1)}, u32[]{:S(2)}, u32[]{:S(2)}) collective-permute-start(bf16[2,48,2048]{2,1,0:T(8,128)(2,1)S(1)} %collective-permute-done.1), channel_id=1, source_target_pairs={{0,240},{16,0},{32,16},{48,32},{64,48},{80,64},{96,80},{112,96},{1... | collective-permute-start | bytes 1179656 | tf_op jit(solution)/shard_map/ppermute | solution.py:38
  53.4 8.4 %collective-permute-start.4 = (bf16[2,48,2048]{2,1,0:T(8,128)(2,1)S(1)}, bf16[2,48,2048]{2,1,0:T(8,128)(2,1)S(1)}, u32[]{:S(2)}, u32[]{:S(2)}) collective-permute-start(bf16[2,48,2048]{2,1,0:T(8,128)(2,1)S(1)} %collective-permute-done.2), channel_id=1, source_target_pairs={{0,16},{16,32},{32,48},{48,64},{64,80},{80,96},{96,112},{112,128},... | collective-permute-start | bytes 1179656 | tf_op jit(solution)/shard_map/ppermute | solution.py:35
  53.4 8.4 %collective-permute-start.5 = (bf16[2,48,2048]{2,1,0:T(8,128)(2,1)S(1)}, bf16[2,48,2048]{2,1,0:T(8,128)(2,1)S(1)}, u32[]{:S(2)}, u32[]{:S(2)}) collective-permute-start(bf16[2,48,2048]{2,1,0:T(8,128)(2,1)S(1)} %collective-permute-done.3), channel_id=1, source_target_pairs={{0,240},{16,0},{32,16},{48,32},{64,48},{80,64},{96,80},{112,96},{1... | collective-permute-start | bytes 1179656 | tf_op jit(solution)/shard_map/ppermute | solution.py:38
  61.8 8.4 %collective-permute-start.6 = (bf16[2,48,2048]{2,1,0:T(8,128)(2,1)S(1)}, bf16[2,48,2048]{2,1,0:T(8,128)(2,1)S(1)}, u32[]{:S(2)}, u32[]{:S(2)}) collective-permute-start(bf16[2,48,2048]{2,1,0:T(8,128)(2,1)S(1)} %collective-permute-done.4), channel_id=1, source_target_pairs={{0,16},{16,32},{32,48},{48,64},{64,80},{80,96},{96,112},{112,128},... | collective-permute-start | bytes 1179656 | tf_op jit(solution)/shard_map/ppermute | solution.py:35
  61.8 8.7 %collective-permute-start.7 = (bf16[2,48,2048]{2,1,0:T(8,128)(2,1)S(1)}, bf16[2,48,2048]{2,1,0:T(8,128)(2,1)S(1)}, u32[]{:S(2)}, u32[]{:S(2)}) collective-permute-start(bf16[2,48,2048]{2,1,0:T(8,128)(2,1)S(1)} %collective-permute-done.5), channel_id=1, source_target_pairs={{0,240},{16,0},{32,16},{48,32},{64,48},{80,64},{96,80},{112,96},{1... | collective-permute-start | bytes 1179656 | tf_op jit(solution)/shard_map/ppermute | solution.py:38
  70.2 8.4 %collective-permute-start.8 = (bf16[2,48,2048]{2,1,0:T(8,128)(2,1)S(1)}, bf16[2,48,2048]{2,1,0:T(8,128)(2,1)S(1)}, u32[]{:S(2)}, u32[]{:S(2)}) collective-permute-start(bf16[2,48,2048]{2,1,0:T(8,128)(2,1)S(1)} %collective-permute-done.6), channel_id=1, source_target_pairs={{0,16},{16,32},{32,48},{48,64},{64,80},{80,96},{96,112},{112,128},... | collective-permute-start | bytes 1179656 | tf_op jit(solution)/shard_map/ppermute | solution.py:35
  70.4 8.8 %collective-permute-start.9 = (bf16[2,48,2048]{2,1,0:T(8,128)(2,1)S(1)}, bf16[2,48,2048]{2,1,0:T(8,128)(2,1)S(1)}, u32[]{:S(2)}, u32[]{:S(2)}) collective-permute-start(bf16[2,48,2048]{2,1,0:T(8,128)(2,1)S(1)} %collective-permute-done.7), channel_id=1, source_target_pairs={{0,240},{16,0},{32,16},{48,32},{64,48},{80,64},{96,80},{112,96},{1... | collective-permute-start | bytes 1179656 | tf_op jit(solution)/shard_map/ppermute | solution.py:38
  78.6 8.4 %collective-permute-start.10 = (bf16[2,48,2048]{2,1,0:T(8,128)(2,1)S(1)}, bf16[2,48,2048]{2,1,0:T(8,128)(2,1)S(1)}, u32[]{:S(2)}, u32[]{:S(2)}) collective-permute-start(bf16[2,48,2048]{2,1,0:T(8,128)(2,1)S(1)} %collective-permute-done.8), channel_id=1, source_target_pairs={{0,16},{16,32},{32,48},{48,64},{64,80},{80,96},{96,112},{112,128},... | collective-permute-start | bytes 1179656 | tf_op jit(solution)/shard_map/ppermute | solution.py:35
  79.2 8.8 %collective-permute-start.11 = (bf16[2,48,2048]{2,1,0:T(8,128)(2,1)S(1)}, bf16[2,48,2048]{2,1,0:T(8,128)(2,1)S(1)}, u32[]{:S(2)}, u32[]{:S(2)}) collective-permute-start(bf16[2,48,2048]{2,1,0:T(8,128)(2,1)S(1)} %collective-permute-done.9), channel_id=1, source_target_pairs={{0,240},{16,0},{32,16},{48,32},{64,48},{80,64},{96,80},{112,96},{1... | collective-permute-start | bytes 1179656 | tf_op jit(solution)/shard_map/ppermute | solution.py:38
  87.0 8.4 %collective-permute-start.12 = (bf16[2,48,2048]{2,1,0:T(8,128)(2,1)S(1)}, bf16[2,48,2048]{2,1,0:T(8,128)(2,1)S(1)}, u32[]{:S(2)}, u32[]{:S(2)}) collective-permute-start(bf16[2,48,2048]{2,1,0:T(8,128)(2,1)S(1)} %collective-permute-done.10), channel_id=1, source_target_pairs={{0,16},{16,32},{32,48},{48,64},{64,80},{80,96},{96,112},{112,128},... | collective-permute-start | bytes 1179656 | tf_op jit(solution)/shard_map/ppermute | solution.py:35
  88.1 8.8 %collective-permute-start.13 = (bf16[2,48,2048]{2,1,0:T(8,128)(2,1)S(1)}, bf16[2,48,2048]{2,1,0:T(8,128)(2,1)S(1)}, u32[]{:S(2)}, u32[]{:S(2)}) collective-permute-start(bf16[2,48,2048]{2,1,0:T(8,128)(2,1)S(1)} %collective-permute-done.11), channel_id=1, source_target_pairs={{0,240},{16,0},{32,16},{48,32},{64,48},{80,64},{96,80},{112,96},{1... | collective-permute-start | bytes 1179656 | tf_op jit(solution)/shard_map/ppermute | solution.py:38
  95.4 8.4 %collective-permute-start.14 = (bf16[2,48,2048]{2,1,0:T(8,128)(2,1)S(1)}, bf16[2,48,2048]{2,1,0:T(8,128)(2,1)S(1)}, u32[]{:S(2)}, u32[]{:S(2)}) collective-permute-start(bf16[2,48,2048]{2,1,0:T(8,128)(2,1)S(1)} %collective-permute-done.12), channel_id=1, source_target_pairs={{0,16},{16,32},{32,48},{48,64},{64,80},{80,96},{96,112},{112,128},... | collective-permute-start | bytes 1179656 | tf_op jit(solution)/shard_map/ppermute | solution.py:35
  141.5 5.8 %copy-start.4 = (f32[128,8]{0,1:T(8,128)S(1)}, f32[128,8]{0,1:T(8,128)}, u32[]{:S(2)}) copy-start(f32[128,8]{0,1:T(8,128)} %param.8) | copy-start | bytes 12292
  141.5 5.9 %copy-start.3 = (s32[128,8]{0,1:T(8,128)S(1)}, s32[128,8]{0,1:T(8,128)}, u32[]{:S(2)}) copy-start(s32[128,8]{0,1:T(8,128)} %param.7) | copy-start | bytes 12292
  141.5 40.5 %all-to-all-start = ((bf16[1,2,1024,768]{3,1,0,2:T(2,128)(2,1)}), bf16[1,2,1024,768]{3,1,0,2:T(2,128)(2,1)S(1)}, u32[]{:S(2)}, u32[]{:S(2)}) async-start(bf16[1,2,1024,768]{3,1,0,2:T(2,128)(2,1)} %copy.32), calls=%async_computation | async-start | bytes 6291456 | tf_op jit(solution)/shard_map/all_to_all | solution.py:82
  147.1 169.5 %reduce-scatter.5.cloned.1.call-start = ((), (), s32[]{:S(2)}) async-start(), calls=%async_computation.6 | async-start | bytes 3342336 | tf_op jit(solution)/shard_map/reduce_scatter | solution.py:95
  182.0 1.7 copy-start.1
  206.1 41.5 %slice-start = ((s8[8388608]{0:T(1024)(128)(4,1)}), s8[4194304]{0:T(1024)(128)(4,1)S(1)}, s32[]{:S(2)}) async-start(s8[8388608]{0:T(1024)(128)(4,1)} %bitcast.56), calls=%async_computation.7 | async-start | bytes 8388608
  208.3 39.3 %slice-start.1 = ((s8[8388608]{0:T(1024)(128)(4,1)}), s8[4194304]{0:T(1024)(128)(4,1)S(1)}, s32[]{:S(2)}) async-start(s8[8388608]{0:T(1024)(128)(4,1)} %bitcast.56), calls=%async_computation.8 | async-start | bytes 8388608
  252.5 126.2 %reduce-scatter.3.cloned.1.call-start = ((), (), s32[]{:S(2)}) async-start(), calls=%async_computation.5 | async-start | bytes 3342336 | tf_op jit(solution)/shard_map/reduce_scatter | solution.py:95
  259.7 1.4 copy-start
Sparse Core Ops, SparseCore 0:
  10.4 78.9 all-gather.2
  252.7 63.9 reduce-scatter.4
  319.2 59.4 reduce-scatter.2
